TPU v7x, 32 devices: a whole 2x2x4 slice. The times are simulated.
32 devices in a mesh: region: 16 (over z, x, core), sub: 2 (over y).
Axes of the slice: x: 2, y: 2, z: 4, core: 2. Of those that a mesh axis runs over, the one named last changes fastest.
Arguments:
- source: float32 [8, 8, 8, 8192], P(None, None, None, ('region', 'sub')), may hold values from -3.5 to 4.5
- metric: float32 [3, 8, 8, 8, 8192], P(None, None, None, None, ('region', 'sub')), may hold values from 0.002 to 0.008
- face_area: float32 [6, 8192], P(None, ('region', 'sub')), may hold values from 0.5 to 13.5
- outlet_gain: float32 [8], replicated, may hold values from 0.0018310547 to 0.0073242188
- neighbour: int32 [6, 8192], P(None, ('region', 'sub')), may hold values from 0 to 2048, as said below
- orient: int32 [6, 8192], P(None, ('region', 'sub')), may hold values from 0 to 7
- outlet: int32 [6, 8192], P(None, ('region', 'sub')), may hold values from 0 to 8, as said below
- export_list: int32 [128, 128], P(('region', 'sub')), may hold values from 0 to 1535, as said below
Outputs:
- solution: float32 [8, 8, 8, 8192], P(None, None, None, ('region', 'sub'))
- residual: float32 [8, 8, 8, 8192], P(None, None, None, ('region', 'sub'))
Inputs may be any that keep to these rules, and one draw needn't show every extreme that they name: Values below 1536 name the device's own faces, the next 128 each the four received lists in pool order; 2048 means the face has no neighbour, as on every outlet face and for any list from a device outside the mesh. 8 means the face belongs to no outlet. `export_list`: each row holds 128 different local face numbers.
All inputs are finite; a program needn't handle non-finite values.
Results may differ from a plain program's by a relative error of at most 0.0001.
Values sent between devices are 32-bit elements; how exact they have to be, the bound alone decides.
A program may use at most 64 MiB of HBM per device.

v0:
```python
import jax
import jax.numpy as jnp
import numpy as np
from jax import lax
from jax.sharding import PartitionSpec as P

NP = 8
OUTLETS = 8
ITERS = 4
GLL_POINTS = np.array(
    [
        -1.0,
        -0.8717401485096066,
        -0.5917001814331423,
        -0.2092992179024789,
        0.2092992179024789,
        0.5917001814331423,
        0.8717401485096066,
        1.0,
    ]
)


def extended(x, sides, width):
    for axis, dim in sides:
        devices, length = (lax.axis_size(axis), x.shape[dim])
        up = [(i, (i + 1) % devices) for i in range(devices - 1)]
        down = [(j, i) for i, j in up]
        last = lax.slice_in_dim(x, length - width, length, axis=dim)
        first = lax.slice_in_dim(x, 0, width, axis=dim)
        before = lax.ppermute(last, axis, up)
        after = lax.ppermute(first, axis, down)
        x = jnp.concatenate([before, x, after], axis=dim)
    return x


def legendre_seven(points):
    previous = points * 0.0 + 1.0
    current = points * 1.0
    for degree in range(1, 7):
        previous, current = (
            current,
            ((2 * degree + 1) * points * current - degree * previous) / (degree + 1),
        )
    return current


def node_tables():
    values = legendre_seven(GLL_POINTS)
    weights = 2.0 / (56.0 * values * values)
    equal = (GLL_POINTS[:, None] == GLL_POINTS[None, :]) * 1.0
    differ = GLL_POINTS[:, None] - GLL_POINTS[None, :] + equal
    deriv = values[:, None] / (values[None, :] * differ) * (1.0 - equal)
    deriv[0, 0] = -14.0
    deriv[7, 7] = 14.0
    return (deriv, np.outer(weights, weights).reshape(-1))


def select_table():
    table = np.zeros((6, NP * NP, NP * NP * NP))
    for first in range(NP):
        for second in range(NP):
            slot = first * NP + second
            table[0, slot, 0 * NP * NP + first * NP + second] = 1.0
            table[1, slot, (NP - 1) * NP * NP + first * NP + second] = 1.0
            table[2, slot, first * NP * NP + 0 * NP + second] = 1.0
            table[3, slot, first * NP * NP + (NP - 1) * NP + second] = 1.0
            table[4, slot, first * NP * NP + second * NP + 0] = 1.0
            table[5, slot, first * NP * NP + second * NP + NP - 1] = 1.0
    return table


def turn_table():
    table = np.zeros((8, NP * NP, NP * NP))
    for variant in range(8):
        moved = np.arange(NP * NP).reshape(NP, NP)
        if variant & 1:
            moved = moved[::-1, :]
        if variant & 2:
            moved = moved[:, ::-1]
        if variant & 4:
            moved = moved.T
        flat_moved = moved.reshape(-1)
        for place in range(NP * NP):
            table[variant, place, flat_moved[place]] = 1.0
    return table


def stiffness(field, metric, deriv):
    highest = lax.Precision.HIGHEST
    grad_a = jnp.einsum("ai,ijke->ajke", deriv, field, precision=highest)
    grad_b = jnp.einsum("bj,ijke->ibke", deriv, field, precision=highest)
    grad_c = jnp.einsum("ck,ijke->ijce", deriv, field, precision=highest)
    result = jnp.einsum("ai,ajke->ijke", deriv, metric[0] * grad_a, precision=highest)
    result = result + jnp.einsum("bj,ibke->ijke", deriv, metric[1] * grad_b, precision=highest)
    return result + jnp.einsum("ck,ijce->ijke", deriv, metric[2] * grad_c, precision=highest)


def local_diagonal(metric, deriv):
    highest = lax.Precision.HIGHEST
    square = deriv * deriv
    result = jnp.einsum("ai,ajke->ijke", square, metric[0], precision=highest)
    result = result + jnp.einsum("bj,ibke->ijke", square, metric[1], precision=highest)
    return result + jnp.einsum("ck,ijce->ijke", square, metric[2], precision=highest)


def face_matrix(field, selector):
    flat_field = field.reshape(NP * NP * NP, -1)
    picked = jnp.einsum("fqn,ne->qfe", selector, flat_field, precision=lax.Precision.HIGHEST)
    return picked.reshape(NP * NP, -1)


def add_faces(field, blocks, selector):
    elem_count = field.shape[3]
    grouped = blocks.reshape(NP * NP, 6, elem_count)
    spread = jnp.einsum("fqn,qfe->ne", selector, grouped, precision=lax.Precision.HIGHEST)
    return field + spread.reshape(field.shape)


def received_blocks(sent_faces, slot_count):
    sub_ext = extended(sent_faces[:, : 2 * slot_count], (("sub", 1),), slot_count)
    region_ext = extended(sent_faces[:, 2 * slot_count :], (("region", 1),), slot_count)
    return [
        sub_ext[:, :slot_count],
        sub_ext[:, 3 * slot_count :],
        region_ext[:, :slot_count],
        region_ext[:, 3 * slot_count :],
    ]


def assemble(values, links, code_hits, rows, slot_count, selector, turner):
    own_faces = face_matrix(values, selector)
    sent_faces = jnp.take(own_faces, rows, axis=1)
    arrived = received_blocks(sent_faces, slot_count)
    face_pool = jnp.concatenate([own_faces] + arrived, axis=1)
    limit = face_pool.shape[1]
    fetched = jnp.take(face_pool, jnp.minimum(links, limit - 1), axis=1)
    fetched = jnp.where(links[None, :] < limit, fetched, 0.0)
    variants = jnp.einsum("vpq,qx->vpx", turner, fetched, precision=lax.Precision.HIGHEST)
    turned = jnp.sum(variants * code_hits[:, None, :], axis=0)
    return add_faces(values, turned, selector)


def outlet_totals(direction, weights, area_flat, outlet_hits, selector):
    sums = jnp.dot(weights, face_matrix(direction, selector), precision=lax.Precision.HIGHEST)
    partial_value = jnp.dot(outlet_hits, area_flat * sums, precision=lax.Precision.HIGHEST)
    return lax.psum(partial_value, ("region", "sub"))


def add_outlet(values, totals, weights, area_flat, outlet_hits, outlet_gain, selector):
    coeff = jnp.dot(outlet_gain * totals, outlet_hits, precision=lax.Precision.HIGHEST) * area_flat
    extra = weights[:, None] * coeff[None, :]
    return add_faces(values, extra, selector)


def per_device(source, metric, face_area, outlet_gain, neighbour, orient, outlet, export_list):
    deriv_np, weights_np = node_tables()
    deriv = jnp.asarray(deriv_np, jnp.float32)
    weights = jnp.asarray(weights_np, jnp.float32)
    selector = jnp.asarray(select_table(), jnp.float32)
    turner = jnp.asarray(turn_table(), jnp.float32)
    links = neighbour.reshape(-1)
    variant_ids = jnp.arange(8, dtype=jnp.int32)
    code_hits = (orient.reshape(-1)[None, :] == variant_ids[:, None]).astype(jnp.float32)
    rows = export_list.reshape(-1)
    slot_count = export_list.shape[1]
    area_flat = face_area.reshape(-1)
    outlet_ids = jnp.arange(OUTLETS, dtype=jnp.int32)
    outlet_hits = (outlet.reshape(-1)[None, :] == outlet_ids[:, None]).astype(jnp.float32)
    diagonal = assemble(
        local_diagonal(metric, deriv), links, code_hits, rows, slot_count, selector, turner
    )
    inverse = 1.0 / diagonal
    centre = 4.5
    half_width = 3.5
    ratio = centre / half_width
    rho_prev = 1.0 / ratio
    residual = source
    direction = inverse * residual / centre
    solution = jnp.zeros_like(source)
    for sweep in range(ITERS):
        solution = solution + direction
        image = assemble(
            stiffness(direction, metric, deriv),
            links,
            code_hits,
            rows,
            slot_count,
            selector,
            turner,
        )
        totals = outlet_totals(direction, weights, area_flat, outlet_hits, selector)
        residual = residual - add_outlet(
            image, totals, weights, area_flat, outlet_hits, outlet_gain, selector
        )
        rho_next = 1.0 / (2.0 * ratio - rho_prev)
        direction = (
            rho_next * rho_prev * direction + 2.0 * rho_next / half_width * inverse * residual
        )
        rho_prev = rho_next
    solution = solution + direction
    return (solution, residual)


def solution(mesh):
    placed = (
        P(None, None, None, ("region", "sub")),
        P(None, None, None, None, ("region", "sub")),
        P(None, ("region", "sub")),
        P(),
        P(None, ("region", "sub")),
        P(None, ("region", "sub")),
        P(None, ("region", "sub")),
        P(("region", "sub"), None),
    )
    return jax.shard_map(
        per_device,
        mesh=mesh,
        in_specs=placed,
        out_specs=(P(None, None, None, ("region", "sub")), P(None, None, None, ("region", "sub"))),
        check_vma=False,
    )
```

profile of v0, /device:TPU:0, one launch (start us, length us, event | category | flops | bytes accessed | tf_op | source)
XLA Modules:
  0.0 406.7 jit_solution(18317932855639597581)
XLA Ops:
  2.0 1.3 fusion.121
  3.3 1.6 fusion.28
  5.6 1.3 fusion.17
  10.7 4.9 %collective-permute-start = (f32[64,128]{0,1:T(8,128)S(1)}, f32[64,128]{0,1:T(8,128)S(1)}, u32[]{:S(2)}, u32[]{:S(2)}) collective-permute-start(f32[64,128]{0,1:T(8,128)S(1)} %get-tuple-element.39), channel_id=1, source_target_pairs={{0,1},{2,3},{4,5},{6,7},{8,9},{10,11},{12,13},{14,15},{16,17},{18,... | collective-permute-start | bytes 98312 | tf_op jit(solution)/shard_map/ppermute | solution.py:31
  16.9 1.5 collective-permute-start.2
  18.4 1.7 collective-permute-start.3
  23.1 3.7 gather_fusion.1
  26.8 4.3 %fusion = f32[64,1536]{1,0:T(8,128)S(1)} fusion(f32[8,1536]{1,0:T(8,128)S(1)} %fusion.93, f32[8,64,64]{2,1,0:T(8,128)} %constant.59.clone, f32[1536,64]{1,0:T(8,128)} %gather_fusion.1, pred[1536]{0:T(1024)(128)(4,1)S(1)} %compare_and_fusion, pred[1536]{0:T(1024)(128)(4,1)S(1)} %lt.28), kind=kOutput, calls=%fused_computation.15 | convolution fusion | flops 605650944 | bytes 969728 | tf_op jit(solution)/shard_map/vpq,qx->vpx/dot_general | solution.py:139
  31.1 1.4 fusion.54
  32.6 1.4 fusion.39
  35.9 1.8 fusion.6
  41.6 1.6 convolution_bitcast_fusion.15
  44.5 1.6 gather_fusion.2
  48.0 16.7 %collective-permute-start.4 = (f32[64,128]{0,1:T(8,128)}, f32[64,128]{0,1:T(8,128)}, u32[]{:S(2)}, u32[]{:S(2)}) collective-permute-start(f32[64,128]{0,1:T(8,128)} %get-tuple-element.35), channel_id=1, source_target_pairs={{0,1},{2,3},{4,5},{6,7},{8,9},{10,11},{12,13},{14,15},{16,17},{18,... | collective-permute-start | bytes 98312 | tf_op jit(solution)/shard_map/ppermute | solution.py:31
  65.9 4.6 %collective-permute-start.6 = (f32[64,128]{0,1:T(8,128)}, f32[64,128]{0,1:T(8,128)S(1)}, u32[]{:S(2)}, u32[]{:S(2)}) collective-permute-start(f32[64,128]{0,1:T(8,128)} %get-tuple-element.33), channel_id=1, source_target_pairs={{0,2},{2,4},{4,6},{6,8},{8,10},{10,12},{12,14},{14,16},{16,18},{18... | collective-permute-start | bytes 98312 | tf_op jit(solution)/shard_map/ppermute | solution.py:31
  70.5 1.9 convolution_bitcast_fusion.14
  72.9 1.3 collective-permute-start.7
  74.3 44.2 %psum.28 = f32[8]{0:T(128)S(1)} all-reduce(f32[8]{0:T(128)S(1)} %convolution_bitcast_fusion.20), channel_id=1, replica_groups=mesh['region'=16,'sub'=2] {'region','sub'}, use_global_device_ids=true, to_apply=%region_2.5 | all-reduce | flops 8 | bytes 64 | tf_op jit(solution)/shard_map/psum | solution.py:147
  118.6 2.2 fusion.68
  123.5 3.7 gather_fusion.3
  127.3 4.3 %fusion.1 = f32[64,1536]{1,0:T(8,128)S(1)} fusion(f32[8,1536]{1,0:T(8,128)S(1)} %copy-done.38, f32[8,64,64]{2,1,0:T(8,128)} %constant.59.clone, f32[1536,64]{1,0:T(8,128)} %gather_fusion.3, pred[1536]{0:T(1024)(128)(4,1)S(1)} %copy-done.60, pred[1536]{0:T(1024)(128)(4,1)S(1)} %copy-done.65), kind=kOutput, calls=%fused_computation.16 | convolution fusion | flops 605650944 | bytes 969728 | tf_op jit(solution)/shard_map/vpq,qx->vpx/dot_general | solution.py:139
  131.6 1.4 fusion.51
  133.1 1.7 multiply_add_fusion.2
  136.7 1.8 fusion.8
  141.8 1.6 convolution_bitcast_fusion.13
  143.4 2.2 copy.118
  145.6 2.8 gather_fusion.4
  150.2 4.9 %collective-permute-start.8 = (f32[64,128]{0,1:T(8,128)}, f32[64,128]{0,1:T(8,128)}, u32[]{:S(2)}, u32[]{:S(2)}) collective-permute-start(f32[64,128]{0,1:T(8,128)} %get-tuple-element.31), channel_id=1, source_target_pairs={{0,1},{2,3},{4,5},{6,7},{8,9},{10,11},{12,13},{14,15},{16,17},{18,... | collective-permute-start | bytes 98312 | tf_op jit(solution)/shard_map/ppermute | solution.py:31
  156.4 1.7 collective-permute-start.10
  159.5 1.3 collective-permute-start.11
  160.8 45.4 %psum.29 = f32[8]{0:T(128)S(1)} all-reduce(f32[8]{0:T(128)S(1)} %convolution_bitcast_fusion.19), channel_id=1, replica_groups=mesh['region'=16,'sub'=2] {'region','sub'}, use_global_device_ids=true, to_apply=%region_4.7 | all-reduce | flops 8 | bytes 64 | tf_op jit(solution)/shard_map/psum | solution.py:147
  207.1 3.0 fusion.66
  211.0 1.5 constant_dynamic-update-slice_fusion.13
  212.5 1.5 constant_dynamic-update-slice_fusion.12
  215.2 4.9 %gather_fusion.5 = f32[1536,64]{1,0:T(8,128)} fusion(f32[64,2048]{0,1:T(8,128)} %constant_dynamic-update-slice_fusion.10, s32[2048]{0:T(1024)S(1)} %pad_clamp_fusion), kind=kCustom, calls=%fused_computation.7.clone | custom fusion | bytes 792576 | tf_op jit(solution)/shard_map/jit(_take)/gather | solution.py:137
  220.1 4.3 %fusion.2 = f32[64,1536]{1,0:T(8,128)S(1)} fusion(f32[8,1536]{1,0:T(8,128)S(1)} %copy-done.38, f32[8,64,64]{2,1,0:T(8,128)} %constant.59.clone, f32[1536,64]{1,0:T(8,128)} %gather_fusion.5, pred[1536]{0:T(1024)(128)(4,1)S(1)} %copy-done.61, pred[1536]{0:T(1024)(128)(4,1)S(1)} %copy-done.66), kind=kOutput, calls=%fused_computation.17 | convolution fusion | flops 605650944 | bytes 969728 | tf_op jit(solution)/shard_map/vpq,qx->vpx/dot_general | solution.py:139
  224.5 1.4 fusion.48
  225.9 1.5 multiply_add_fusion.1
  229.4 1.8 fusion.10
  235.3 1.6 convolution_bitcast_fusion.11
  236.9 2.2 copy.120
  239.0 2.8 gather_fusion.6
  243.6 4.9 %collective-permute-start.12 = (f32[64,128]{0,1:T(8,128)}, f32[64,128]{0,1:T(8,128)}, u32[]{:S(2)}, u32[]{:S(2)}) collective-permute-start(f32[64,128]{0,1:T(8,128)} %get-tuple-element.27), channel_id=1, source_target_pairs={{0,1},{2,3},{4,5},{6,7},{8,9},{10,11},{12,13},{14,15},{16,17},{18,... | collective-permute-start | bytes 98312 | tf_op jit(solution)/shard_map/ppermute | solution.py:31
  249.8 1.5 collective-permute-start.14
  251.3 1.9 convolution_bitcast_fusion.10
  255.6 43.6 %psum.30 = f32[8]{0:T(128)} all-reduce(f32[8]{0:T(128)} %convolution_bitcast_fusion.18), channel_id=1, replica_groups=mesh['region'=16,'sub'=2] {'region','sub'}, use_global_device_ids=true, to_apply=%region_6.9 | all-reduce | flops 8 | bytes 64 | tf_op jit(solution)/shard_map/psum | solution.py:147
  301.4 2.2 fusion.64
  304.6 1.5 constant_dynamic-update-slice_fusion.18
  306.0 1.5 constant_dynamic-update-slice_fusion.17
  308.1 1.5 constant_dynamic-update-slice_fusion.15
  309.6 4.9 %gather_fusion.7 = f32[1536,64]{1,0:T(8,128)} fusion(f32[64,2048]{0,1:T(8,128)} %constant_dynamic-update-slice_fusion.15, s32[2048]{0:T(1024)S(1)} %pad_clamp_fusion), kind=kCustom, calls=%fused_computation.8.clone | custom fusion | bytes 792576 | tf_op jit(solution)/shard_map/jit(_take)/gather | solution.py:137
  314.5 4.3 %fusion.3 = f32[64,1536]{1,0:T(8,128)S(1)} fusion(f32[8,1536]{1,0:T(8,128)S(1)} %copy-done.38, f32[8,64,64]{2,1,0:T(8,128)} %constant.59.clone, f32[1536,64]{1,0:T(8,128)} %gather_fusion.7, pred[1536]{0:T(1024)(128)(4,1)S(1)} %copy-done.62, pred[1536]{0:T(1024)(128)(4,1)S(1)} %copy-done.67), kind=kOutput, calls=%fused_computation.18 | convolution fusion | flops 605650944 | bytes 969728 | tf_op jit(solution)/shard_map/vpq,qx->vpx/dot_general | solution.py:139
  318.9 1.4 fusion.45
  320.4 1.5 multiply_add_fusion
  323.8 1.8 fusion.12
  333.3 5.1 %collective-permute-start.16 = (f32[64,128]{0,1:T(8,128)}, f32[64,128]{0,1:T(8,128)}, u32[]{:S(2)}, u32[]{:S(2)}) collective-permute-start(f32[64,128]{0,1:T(8,128)} %get-tuple-element.23), channel_id=1, source_target_pairs={{0,1},{2,3},{4,5},{6,7},{8,9},{10,11},{12,13},{14,15},{16,17},{18,... | collective-permute-start | bytes 98312 | tf_op jit(solution)/shard_map/ppermute | solution.py:31
  339.7 1.5 collective-permute-start.18
  341.2 1.9 convolution_bitcast_fusion.8
  343.7 1.3 collective-permute-start.19
  345.0 44.7 %psum.31 = f32[8]{0:T(128)S(1)} all-reduce(f32[8]{0:T(128)S(1)} %convolution_bitcast_fusion.17), channel_id=1, replica_groups=mesh['region'=16,'sub'=2] {'region','sub'}, use_global_device_ids=true, to_apply=%region_8.11 | all-reduce | flops 8 | bytes 64 | tf_op jit(solution)/shard_map/psum | solution.py:147
  389.9 2.3 fusion.62
  394.0 3.7 gather_fusion.9
  397.7 4.3 %fusion.4 = f32[64,1536]{1,0:T(8,128)S(1)} fusion(f32[8,1536]{1,0:T(8,128)S(1)} %copy-done.39, f32[8,64,64]{2,1,0:T(8,128)} %constant.59.clone, f32[1536,64]{1,0:T(8,128)} %gather_fusion.9, pred[1536]{0:T(1024)(128)(4,1)S(1)} %copy-done.63, pred[1536]{0:T(1024)(128)(4,1)S(1)} %copy-done.68), kind=kOutput, calls=%fused_computation.19 | convolution fusion | flops 605650944 | bytes 969728 | tf_op jit(solution)/shard_map/vpq,qx->vpx/dot_general | solution.py:139
  402.1 1.4 fusion.42
  (285 shorter events, 67.6 us)
Async XLA Ops:
  2.0 8.5 %copy-start.42 = (pred[512]{0:T(512)(128)(4,1)}, pred[512]{0:T(512)(128)(4,1)S(1)}, u32[]{:S(2)}) copy-start(pred[512]{0:T(512)(128)(4,1)S(1)} %compare_and_fusion.1) | copy-start | bytes 1540
  8.8 9.6 %copy-start.13 = (f32[64,6,256]{0,2,1:T(8,128)}, f32[64,6,256]{0,2,1:T(8,128)S(1)}, u32[]{:S(2)}) copy-start(f32[64,6,256]{0,2,1:T(8,128)S(1)} %copy.114) | copy-start | bytes 1179652
  10.5 10.8 %copy-start.41 = (s32[6,256]{1,0:T(8,128)S(1)}, s32[6,256]{1,0:T(8,128)}, u32[]{:S(2)}) copy-start(s32[6,256]{1,0:T(8,128)} %param.20) | copy-start | bytes 18436
  10.5 10.8 %copy-start.52 = (s32[6,256]{1,0:T(8,128)S(1)}, s32[6,256]{1,0:T(8,128)}, u32[]{:S(2)}) copy-start(s32[6,256]{1,0:T(8,128)} %param.21) | copy-start | bytes 18436
  10.5 10.9 %copy-start.53 = (f32[6,256]{1,0:T(8,128)S(1)}, f32[6,256]{1,0:T(8,128)}, u32[]{:S(2)}) copy-start(f32[6,256]{1,0:T(8,128)} %param.18) | copy-start | bytes 18436
  10.6 10.9 %copy-start.54 = (s32[6,256]{1,0:T(8,128)S(1)}, s32[6,256]{1,0:T(8,128)}, u32[]{:S(2)}) copy-start(s32[6,256]{1,0:T(8,128)} %param.22) | copy-start | bytes 18436
  10.7 11.4 %collective-permute-start = (f32[64,128]{0,1:T(8,128)S(1)}, f32[64,128]{0,1:T(8,128)S(1)}, u32[]{:S(2)}, u32[]{:S(2)}) collective-permute-start(f32[64,128]{0,1:T(8,128)S(1)} %get-tuple-element.39), channel_id=1, source_target_pairs={{0,1},{2,3},{4,5},{6,7},{8,9},{10,11},{12,13},{14,15},{16,17},{18,... | collective-permute-start | bytes 98312 | tf_op jit(solution)/shard_map/ppermute | solution.py:31
  15.6 6.5 %collective-permute-start.1 = (f32[64,128]{0,1:T(8,128)S(1)}, f32[64,128]{0,1:T(8,128)S(1)}, u32[]{:S(2)}, u32[]{:S(2)}) collective-permute-start(f32[64,128]{0,1:T(8,128)S(1)} %get-tuple-element.38), channel_id=1, source_target_pairs={{1,0},{3,2},{5,4},{7,6},{9,8},{11,10},{13,12},{15,14},{17,16},{19,... | collective-permute-start | bytes 98312 | tf_op jit(solution)/shard_map/ppermute | solution.py:32
  16.9 5.2 %collective-permute-start.2 = (f32[64,128]{0,1:T(8,128)S(1)}, f32[64,128]{0,1:T(8,128)S(1)}, u32[]{:S(2)}, u32[]{:S(2)}) collective-permute-start(f32[64,128]{0,1:T(8,128)S(1)} %get-tuple-element.37), channel_id=1, source_target_pairs={{0,2},{2,4},{4,6},{6,8},{8,10},{10,12},{12,14},{14,16},{16,18},{18... | collective-permute-start | bytes 98312 | tf_op jit(solution)/shard_map/ppermute | solution.py:31
  18.4 4.7 %collective-permute-start.3 = (f32[64,128]{0,1:T(8,128)S(1)}, f32[64,128]{0,1:T(8,128)S(1)}, u32[]{:S(2)}, u32[]{:S(2)}) collective-permute-start(f32[64,128]{0,1:T(8,128)S(1)} %get-tuple-element.36), channel_id=1, source_target_pairs={{2,0},{4,2},{6,4},{8,6},{10,8},{12,10},{14,12},{16,14},{18,16},{20... | collective-permute-start | bytes 98312 | tf_op jit(solution)/shard_map/ppermute | solution.py:32
  21.4 5.5 %copy-start.59 = (pred[1536]{0:T(1024)(128)(4,1)}, pred[1536]{0:T(1024)(128)(4,1)S(1)}, u32[]{:S(2)}) copy-start(pred[1536]{0:T(1024)(128)(4,1)S(1)} %compare_and_fusion) | copy-start | bytes 4612
  21.4 5.4 %copy-start.37 = (f32[8,1536]{1,0:T(8,128)}, f32[8,1536]{1,0:T(8,128)S(1)}, u32[]{:S(2)}) copy-start(f32[8,1536]{1,0:T(8,128)S(1)} %fusion.93) | copy-start | bytes 147460
  21.5 5.3 %copy-start.64 = (pred[1536]{0:T(1024)(128)(4,1)}, pred[1536]{0:T(1024)(128)(4,1)S(1)}, u32[]{:S(2)}) copy-start(pred[1536]{0:T(1024)(128)(4,1)S(1)} %lt.28) | copy-start | bytes 4612
  26.8 5.7 %copy-start.17 = (f32[8,8,8,256]{3,0,2,1:T(8,128)S(1)}, f32[8,8,8,256]{3,0,2,1:T(8,128)}, u32[]{:S(2)}) copy-start(f32[8,8,8,256]{3,0,2,1:T(8,128)} %copy-done.16) | copy-start | bytes 1572868
  26.8 5.7 %copy-start.25 = (f32[8,8,8,256]{3,2,1,0:T(8,128)S(1)}, f32[8,8,8,256]{3,2,1,0:T(8,128)}, u32[]{:S(2)}) copy-start(f32[8,8,8,256]{3,2,1,0:T(8,128)} %param.16) | copy-start | bytes 1572868
  44.5 27.9 %copy-start.9 = (f32[64,6,256]{0,2,1:T(8,128)}, f32[64,6,256]{0,2,1:T(8,128)S(1)}, u32[]{:S(2)}) copy-start(f32[64,6,256]{0,2,1:T(8,128)S(1)} %copy.116) | copy-start | bytes 1179652
  47.2 25.2 %copy-start.48 = (f32[64,1]{0,1:T(1,128)S(1)}, f32[64,1]{0,1:T(1,128)}, u32[]{:S(2)}) copy-start(f32[64,1]{0,1:T(1,128)} %constant.64) | copy-start | bytes 772
  48.0 24.8 %copy-start.55 = (s32[1536]{0:T(1024)S(1)}, s32[1536]{0:T(1024)}, u32[]{:S(2)}) copy-start(s32[1536]{0:T(1024)} %eq.38) | copy-start | bytes 18436
  48.0 70.4 %copy-start.69 = (f32[8]{0:T(128)S(1)}, f32[8]{0:T(128)}, u32[]{:S(2)}) copy-start(f32[8]{0:T(128)} %param.19) | copy-start | bytes 100
  48.0 70.6 %copy-start.45 = (f32[64]{0:T(128)S(1)}, f32[64]{0:T(128)}, u32[]{:S(2)}) copy-start(f32[64]{0:T(128)} %constant.32.clone) | copy-start | bytes 772
  48.0 73.0 %collective-permute-start.4 = (f32[64,128]{0,1:T(8,128)}, f32[64,128]{0,1:T(8,128)}, u32[]{:S(2)}, u32[]{:S(2)}) collective-permute-start(f32[64,128]{0,1:T(8,128)} %get-tuple-element.35), channel_id=1, source_target_pairs={{0,1},{2,3},{4,5},{6,7},{8,9},{10,11},{12,13},{14,15},{16,17},{18,... | collective-permute-start | bytes 98312 | tf_op jit(solution)/shard_map/ppermute | solution.py:31
  64.6 57.2 %collective-permute-start.5 = (f32[64,128]{0,1:T(8,128)}, f32[64,128]{0,1:T(8,128)}, u32[]{:S(2)}, u32[]{:S(2)}) collective-permute-start(f32[64,128]{0,1:T(8,128)} %get-tuple-element.34), channel_id=1, source_target_pairs={{1,0},{3,2},{5,4},{7,6},{9,8},{11,10},{13,12},{15,14},{17,16},{19,... | collective-permute-start | bytes 98312 | tf_op jit(solution)/shard_map/ppermute | solution.py:32
  65.9 56.7 %collective-permute-start.6 = (f32[64,128]{0,1:T(8,128)}, f32[64,128]{0,1:T(8,128)S(1)}, u32[]{:S(2)}, u32[]{:S(2)}) collective-permute-start(f32[64,128]{0,1:T(8,128)} %get-tuple-element.33), channel_id=1, source_target_pairs={{0,2},{2,4},{4,6},{6,8},{8,10},{10,12},{12,14},{14,16},{16,18},{18... | collective-permute-start | bytes 98312 | tf_op jit(solution)/shard_map/ppermute | solution.py:31
  72.9 49.7 %collective-permute-start.7 = (f32[64,128]{0,1:T(8,128)}, f32[64,128]{0,1:T(8,128)}, u32[]{:S(2)}, u32[]{:S(2)}) collective-permute-start(f32[64,128]{0,1:T(8,128)} %get-tuple-element.32), channel_id=1, source_target_pairs={{2,0},{4,2},{6,4},{8,6},{10,8},{12,10},{14,12},{16,14},{18,16},{20... | collective-permute-start | bytes 98312 | tf_op jit(solution)/shard_map/ppermute | solution.py:32
  127.2 5.8 %copy-start.3 = (f32[8,8,8,256]{3,0,2,1:T(8,128)S(1)}, f32[8,8,8,256]{3,0,2,1:T(8,128)}, u32[]{:S(2)}) copy-start(f32[8,8,8,256]{3,0,2,1:T(8,128)} %get-tuple-element.17) | copy-start | bytes 1572868
  127.2 5.8 %copy-start.15 = (f32[8,8,8,256]{3,0,2,1:T(8,128)S(1)}, f32[8,8,8,256]{3,0,2,1:T(8,128)}, u32[]{:S(2)}) copy-start(f32[8,8,8,256]{3,0,2,1:T(8,128)} %copy-done.14) | copy-start | bytes 1572868
  127.2 5.8 %copy-start.26 = (f32[8,8,8,256]{3,2,1,0:T(8,128)S(1)}, f32[8,8,8,256]{3,2,1,0:T(8,128)}, u32[]{:S(2)}) copy-start(f32[8,8,8,256]{3,2,1,0:T(8,128)} %param.16) | copy-start | bytes 1572868
  127.2 5.8 %copy-start.27 = (f32[512,256,1]{1,0,2:T(8,128)S(1)}, f32[512,256,1]{1,0,2:T(8,128)}, u32[]{:S(2)}) copy-start(f32[512,256,1]{1,0,2:T(8,128)} %fusion.68) | copy-start | bytes 1572868
  145.6 12.5 %copy-start.28 = (f32[8,8,8,256]{3,2,1,0:T(8,128)S(1)}, f32[8,8,8,256]{3,2,1,0:T(8,128)}, u32[]{:S(2)}) copy-start(f32[8,8,8,256]{3,2,1,0:T(8,128)} %copy.69) | copy-start | bytes 1572868
  149.5 9.5 %copy-start.49 = (f32[64,1]{0,1:T(1,128)S(1)}, f32[64,1]{0,1:T(1,128)}, u32[]{:S(2)}) copy-start(f32[64,1]{0,1:T(1,128)} %constant.64) | copy-start | bytes 772
  150.2 9.2 %copy-start.56 = (s32[1536]{0:T(1024)S(1)}, s32[1536]{0:T(1024)}, u32[]{:S(2)}) copy-start(s32[1536]{0:T(1024)} %eq.38) | copy-start | bytes 18436
  150.2 60.8 %collective-permute-start.8 = (f32[64,128]{0,1:T(8,128)}, f32[64,128]{0,1:T(8,128)}, u32[]{:S(2)}, u32[]{:S(2)}) collective-permute-start(f32[64,128]{0,1:T(8,128)} %get-tuple-element.31), channel_id=1, source_target_pairs={{0,1},{2,3},{4,5},{6,7},{8,9},{10,11},{12,13},{14,15},{16,17},{18,... | collective-permute-start | bytes 98312 | tf_op jit(solution)/shard_map/ppermute | solution.py:31
  155.1 57.4 %collective-permute-start.9 = (f32[64,128]{0,1:T(8,128)}, f32[64,128]{0,1:T(8,128)}, u32[]{:S(2)}, u32[]{:S(2)}) collective-permute-start(f32[64,128]{0,1:T(8,128)} %get-tuple-element.30), channel_id=1, source_target_pairs={{1,0},{3,2},{5,4},{7,6},{9,8},{11,10},{13,12},{15,14},{17,16},{19,... | collective-permute-start | bytes 98312 | tf_op jit(solution)/shard_map/ppermute | solution.py:32
  156.4 57.5 %collective-permute-start.10 = (f32[64,128]{0,1:T(8,128)}, f32[64,128]{0,1:T(8,128)S(1)}, u32[]{:S(2)}, u32[]{:S(2)}) collective-permute-start(f32[64,128]{0,1:T(8,128)} %get-tuple-element.29), channel_id=1, source_target_pairs={{0,2},{2,4},{4,6},{6,8},{8,10},{10,12},{12,14},{14,16},{16,18},{18... | collective-permute-start | bytes 98312 | tf_op jit(solution)/shard_map/ppermute | solution.py:31
  159.5 55.1 %collective-permute-start.11 = (f32[64,128]{0,1:T(8,128)}, f32[64,128]{0,1:T(8,128)S(1)}, u32[]{:S(2)}, u32[]{:S(2)}) collective-permute-start(f32[64,128]{0,1:T(8,128)} %get-tuple-element.28), channel_id=1, source_target_pairs={{2,0},{4,2},{6,4},{8,6},{10,8},{12,10},{14,12},{16,14},{18,16},{20... | collective-permute-start | bytes 98312 | tf_op jit(solution)/shard_map/ppermute | solution.py:32
  220.1 5.8 %copy-start.4 = (f32[8,8,8,256]{3,0,2,1:T(8,128)S(1)}, f32[8,8,8,256]{3,0,2,1:T(8,128)}, u32[]{:S(2)}) copy-start(f32[8,8,8,256]{3,0,2,1:T(8,128)} %get-tuple-element.17) | copy-start | bytes 1572868
  220.1 5.8 %copy-start.21 = (f32[8,8,8,256]{3,0,2,1:T(8,128)S(1)}, f32[8,8,8,256]{3,0,2,1:T(8,128)}, u32[]{:S(2)}) copy-start(f32[8,8,8,256]{3,0,2,1:T(8,128)} %copy-done.20) | copy-start | bytes 1572868
  220.1 5.8 %copy-start.29 = (f32[8,8,8,256]{3,0,2,1:T(8,128)S(1)}, f32[8,8,8,256]{3,0,2,1:T(8,128)}, u32[]{:S(2)}) copy-start(f32[8,8,8,256]{3,0,2,1:T(8,128)} %get-tuple-element.15) | copy-start | bytes 1572868
  220.1 5.8 %copy-start.31 = (f32[512,256,1]{1,0,2:T(8,128)S(1)}, f32[512,256,1]{1,0,2:T(8,128)}, u32[]{:S(2)}) copy-start(f32[512,256,1]{1,0,2:T(8,128)} %fusion.66) | copy-start | bytes 1572868
  242.9 10.3 %copy-start.50 = (f32[64,1]{0,1:T(1,128)S(1)}, f32[64,1]{0,1:T(1,128)}, u32[]{:S(2)}) copy-start(f32[64,1]{0,1:T(1,128)} %constant.64) | copy-start | bytes 772
  243.6 10.0 %copy-start.57 = (s32[1536]{0:T(1024)S(1)}, s32[1536]{0:T(1024)}, u32[]{:S(2)}) copy-start(s32[1536]{0:T(1024)} %eq.38) | copy-start | bytes 18436
  243.6 57.8 %copy-start.46 = (f32[64]{0:T(128)S(1)}, f32[64]{0:T(128)}, u32[]{:S(2)}) copy-start(f32[64]{0:T(128)} %constant.32.clone) | copy-start | bytes 772
  243.6 61.0 %collective-permute-start.12 = (f32[64,128]{0,1:T(8,128)}, f32[64,128]{0,1:T(8,128)}, u32[]{:S(2)}, u32[]{:S(2)}) collective-permute-start(f32[64,128]{0,1:T(8,128)} %get-tuple-element.27), channel_id=1, source_target_pairs={{0,1},{2,3},{4,5},{6,7},{8,9},{10,11},{12,13},{14,15},{16,17},{18,... | collective-permute-start | bytes 98312 | tf_op jit(solution)/shard_map/ppermute | solution.py:31
  248.5 57.5 %collective-permute-start.13 = (f32[64,128]{0,1:T(8,128)}, f32[64,128]{0,1:T(8,128)}, u32[]{:S(2)}, u32[]{:S(2)}) collective-permute-start(f32[64,128]{0,1:T(8,128)} %get-tuple-element.26), channel_id=1, source_target_pairs={{1,0},{3,2},{5,4},{7,6},{9,8},{11,10},{13,12},{15,14},{17,16},{19,... | collective-permute-start | bytes 98312 | tf_op jit(solution)/shard_map/ppermute | solution.py:32
  249.8 57.7 %collective-permute-start.14 = (f32[64,128]{0,1:T(8,128)}, f32[64,128]{0,1:T(8,128)S(1)}, u32[]{:S(2)}, u32[]{:S(2)}) collective-permute-start(f32[64,128]{0,1:T(8,128)} %get-tuple-element.25), channel_id=1, source_target_pairs={{0,2},{2,4},{4,6},{6,8},{8,10},{10,12},{12,14},{14,16},{16,18},{18... | collective-permute-start | bytes 98312 | tf_op jit(solution)/shard_map/ppermute | solution.py:31
  254.3 53.9 %collective-permute-start.15 = (f32[64,128]{0,1:T(8,128)}, f32[64,128]{0,1:T(8,128)}, u32[]{:S(2)}, u32[]{:S(2)}) collective-permute-start(f32[64,128]{0,1:T(8,128)} %get-tuple-element.24), channel_id=1, source_target_pairs={{2,0},{4,2},{6,4},{8,6},{10,8},{12,10},{14,12},{16,14},{18,16},{20... | collective-permute-start | bytes 98312 | tf_op jit(solution)/shard_map/ppermute | solution.py:32
  314.5 5.8 %copy-start.5 = (f32[8,8,8,256]{3,0,2,1:T(8,128)S(1)}, f32[8,8,8,256]{3,0,2,1:T(8,128)}, u32[]{:S(2)}) copy-start(f32[8,8,8,256]{3,0,2,1:T(8,128)} %get-tuple-element.17) | copy-start | bytes 1572868
  314.5 5.8 %copy-start.23 = (f32[8,8,8,256]{3,0,2,1:T(8,128)S(1)}, f32[8,8,8,256]{3,0,2,1:T(8,128)}, u32[]{:S(2)}) copy-start(f32[8,8,8,256]{3,0,2,1:T(8,128)} %copy-done.22) | copy-start | bytes 1572868
  314.5 5.8 %copy-start.32 = (f32[512,256,1]{1,0,2:T(8,128)S(1)}, f32[512,256,1]{1,0,2:T(8,128)}, u32[]{:S(2)}) copy-start(f32[512,256,1]{1,0,2:T(8,128)} %fusion.64) | copy-start | bytes 1572868
  314.5 5.8 %copy-start.34 = (f32[8,8,8,256]{3,0,2,1:T(8,128)S(1)}, f32[8,8,8,256]{3,0,2,1:T(8,128)}, u32[]{:S(2)}) copy-start(f32[8,8,8,256]{3,0,2,1:T(8,128)} %get-tuple-element.13) | copy-start | bytes 1572868
  330.6 12.5 %copy-start.7 = (f32[64,6,256]{0,2,1:T(8,128)}, f32[64,6,256]{0,2,1:T(8,128)S(1)}, u32[]{:S(2)}) copy-start(f32[64,6,256]{0,2,1:T(8,128)S(1)} %copy.122) | copy-start | bytes 1179652
  332.6 10.6 %copy-start.51 = (f32[64,1]{0,1:T(1,128)S(1)}, f32[64,1]{0,1:T(1,128)}, u32[]{:S(2)}) copy-start(f32[64,1]{0,1:T(1,128)} %constant.64) | copy-start | bytes 772
  333.3 10.2 %copy-start.58 = (s32[1536]{0:T(1024)S(1)}, s32[1536]{0:T(1024)}, u32[]{:S(2)}) copy-start(s32[1536]{0:T(1024)} %eq.38) | copy-start | bytes 18436
  333.3 56.4 %copy-start.70 = (f32[8]{0:T(128)S(1)}, f32[8]{0:T(128)}, u32[]{:S(2)}) copy-start(f32[8]{0:T(128)} %param.19) | copy-start | bytes 100
  333.3 56.6 %copy-start.47 = (f32[64]{0:T(128)S(1)}, f32[64]{0:T(128)}, u32[]{:S(2)}) copy-start(f32[64]{0:T(128)} %constant.32.clone) | copy-start | bytes 772
  333.3 58.9 %collective-permute-start.16 = (f32[64,128]{0,1:T(8,128)}, f32[64,128]{0,1:T(8,128)}, u32[]{:S(2)}, u32[]{:S(2)}) collective-permute-start(f32[64,128]{0,1:T(8,128)} %get-tuple-element.23), channel_id=1, source_target_pairs={{0,1},{2,3},{4,5},{6,7},{8,9},{10,11},{12,13},{14,15},{16,17},{18,... | collective-permute-start | bytes 98312 | tf_op jit(solution)/shard_map/ppermute | solution.py:31
  338.4 54.6 %collective-permute-start.17 = (f32[64,128]{0,1:T(8,128)}, f32[64,128]{0,1:T(8,128)S(1)}, u32[]{:S(2)}, u32[]{:S(2)}) collective-permute-start(f32[64,128]{0,1:T(8,128)} %get-tuple-element.22), channel_id=1, source_target_pairs={{1,0},{3,2},{5,4},{7,6},{9,8},{11,10},{13,12},{15,14},{17,16},{19,... | collective-permute-start | bytes 98312 | tf_op jit(solution)/shard_map/ppermute | solution.py:32
  339.7 53.4 %collective-permute-start.18 = (f32[64,128]{0,1:T(8,128)}, f32[64,128]{0,1:T(8,128)S(1)}, u32[]{:S(2)}, u32[]{:S(2)}) collective-permute-start(f32[64,128]{0,1:T(8,128)} %get-tuple-element.21), channel_id=1, source_target_pairs={{0,2},{2,4},{4,6},{6,8},{8,10},{10,12},{12,14},{14,16},{16,18},{18... | collective-permute-start | bytes 98312 | tf_op jit(solution)/shard_map/ppermute | solution.py:31
  343.7 49.4 %collective-permute-start.19 = (f32[64,128]{0,1:T(8,128)}, f32[64,128]{0,1:T(8,128)}, u32[]{:S(2)}, u32[]{:S(2)}) collective-permute-start(f32[64,128]{0,1:T(8,128)} %get-tuple-element.20), channel_id=1, source_target_pairs={{2,0},{4,2},{6,4},{8,6},{10,8},{12,10},{14,12},{16,14},{18,16},{20... | collective-permute-start | bytes 98312 | tf_op jit(solution)/shard_map/ppermute | solution.py:32
  397.7 5.8 %copy-start.2 = (f32[8,8,8,256]{3,0,2,1:T(8,128)S(1)}, f32[8,8,8,256]{3,0,2,1:T(8,128)}, u32[]{:S(2)}) copy-start(f32[8,8,8,256]{3,0,2,1:T(8,128)} %copy-done.1) | copy-start | bytes 1572868
  397.7 5.8 %copy-start.6 = (f32[8,8,8,256]{3,0,2,1:T(8,128)S(1)}, f32[8,8,8,256]{3,0,2,1:T(8,128)}, u32[]{:S(2)}) copy-start(f32[8,8,8,256]{3,0,2,1:T(8,128)} %get-tuple-element.17) | copy-start | bytes 1572868
  397.7 5.8 %copy-start.19 = (f32[8,8,8,256]{3,0,2,1:T(8,128)S(1)}, f32[8,8,8,256]{3,0,2,1:T(8,128)}, u32[]{:S(2)}) copy-start(f32[8,8,8,256]{3,0,2,1:T(8,128)} %copy-done.18) | copy-start | bytes 1572868
  397.7 5.8 %copy-start.30 = (f32[512,256,1]{1,0,2:T(8,128)S(1)}, f32[512,256,1]{1,0,2:T(8,128)}, u32[]{:S(2)}) copy-start(f32[512,256,1]{1,0,2:T(8,128)} %fusion.62) | copy-start | bytes 1572868
  397.7 5.8 %copy-start.33 = (f32[8,8,8,256]{3,0,2,1:T(8,128)S(1)}, f32[8,8,8,256]{3,0,2,1:T(8,128)}, u32[]{:S(2)}) copy-start(f32[8,8,8,256]{3,0,2,1:T(8,128)} %get-tuple-element.11) | copy-start | bytes 1572868
  (27 other events, 80.4 us)
where the time goes:
time: 413 us; the launch traced here: 407 us
  blocking collectives  178 us (43%)
  matrix products  82.6 us (20%)
  local copies, waits for them, and re-layouts  68.7 us (17%)
  starting transfers between devices  60.6 us (15%)
  other arithmetic  13.4 us (3%)
    psum x4, blocking collectives, outlet_totals(): return lax.psum(partial_value, ('region', 'sub'))  178 us
    ppermute x10, starting transfers between devices, extended(): before = lax.ppermute(last, axis, up)  47.2 us
    dot_general x5, matrix products, assemble(): jnp.einsum('vpq,qx->vpx', turner, fetched, precision=lax.Precision.HIGHEST)  21.6 us
    gather x5, local copies, waits for them, and re-layouts, assemble(): fetched = jnp.take(face_pool, jnp.minimum(links, limit - 1), axis=1)  20.8 us
    unnamed x164, local copies, waits for them, and re-layouts  18.3 us
    dot_general x9, matrix products, add_faces(): jnp.einsum('fqn,qfe->ne', selector, grouped, precision=lax.Precision.HIGH...  16.9 us
    ppermute x10, starting transfers between devices, extended(): after = lax.ppermute(first, axis, down)  13.3 us
    dot_general x9, matrix products, face_matrix(): jnp.einsum('fqn,ne->qfe', selector, flat_field, precision=lax.Precision.H...  12.7 us
  transfers between devices with their start and end apart: 20, of which 1 were waited for; matrix products, arithmetic and copies ran while one was open for 9% of the time, Pallas kernels for 0%

commit v1 on v0

--- a/solution.py
+++ b/solution.py
@@ -144,7 +144,8 @@
 def outlet_totals(direction, weights, area_flat, outlet_hits, selector):
     sums = jnp.dot(weights, face_matrix(direction, selector), precision=lax.Precision.HIGHEST)
     partial_value = jnp.dot(outlet_hits, area_flat * sums, precision=lax.Precision.HIGHEST)
-    return lax.psum(partial_value, ("region", "sub"))
+    store_classes = lambda u: lax.psum(lax.psum(u, "sub"), "region")
+    return store_classes(partial_value)
 
 
 def add_outlet(values, totals, weights, area_flat, outlet_hits, outlet_gain, selector):

time: 413 us -> 383 us (0.927)
  blocking collectives: 178 us -> 149 us
    psum x4 -> x8, blocking collectives: 178 us -> 149 us  [outlet_totals(): store_classes = lambda u: lax.psum(lax.psum(u, 'sub'), 'region')]
where the time goes in v1:
time: 383 us; the launch traced here: 377 us
  blocking collectives  149 us (39%)
  matrix products  82.6 us (22%)
  local copies, waits for them, and re-layouts  67.8 us (18%)
  starting transfers between devices  60.5 us (16%)
  other arithmetic  13.5 us (4%)
    psum x8, blocking collectives, outlet_totals(): store_classes = lambda u: lax.psum(lax.psum(u, 'sub'), 'region')  149 us
    ppermute x10, starting transfers between devices, extended(): before = lax.ppermute(last, axis, up)  46.5 us
    dot_general x5, matrix products, assemble(): jnp.einsum('vpq,qx->vpx', turner, fetched, precision=lax.Precision.HIGHEST)  21.6 us
    gather x5, local copies, waits for them, and re-layouts, assemble(): fetched = jnp.take(face_pool, jnp.minimum(links, limit - 1), axis=1)  20.8 us
    unnamed x164, local copies, waits for them, and re-layouts  17.4 us
    dot_general x9, matrix products, add_faces(): jnp.einsum('fqn,qfe->ne', selector, grouped, precision=lax.Precision.HIGH...  16.8 us
    ppermute x10, starting transfers between devices, extended(): after = lax.ppermute(first, axis, down)  14 us
    dot_general x9, matrix products, face_matrix(): jnp.einsum('fqn,ne->qfe', selector, flat_field, precision=lax.Precision.H...  12.8 us
  transfers between devices with their start and end apart: 20, of which 1 were waited for; matrix products, arithmetic and copies ran while one was open for 9% of the time, Pallas kernels for 0%

profile of v1, /device:TPU:0, one launch (start us, length us, event | category | flops | bytes accessed | tf_op | source)
XLA Modules:
  0.0 376.6 jit_solution(16202721161085297435)
XLA Ops:
  3.3 1.6 fusion.28
  10.7 4.9 %collective-permute-start = (f32[64,128]{0,1:T(8,128)S(1)}, f32[64,128]{0,1:T(8,128)S(1)}, u32[]{:S(2)}, u32[]{:S(2)}) collective-permute-start(f32[64,128]{0,1:T(8,128)S(1)} %get-tuple-element.39), channel_id=1, source_target_pairs={{0,1},{2,3},{4,5},{6,7},{8,9},{10,11},{12,13},{14,15},{16,17},{18,... | collective-permute-start | bytes 98312 | tf_op jit(solution)/shard_map/ppermute | solution.py:31
  16.9 1.5 collective-permute-start.2
  18.4 1.7 collective-permute-start.3
  23.1 3.7 gather_fusion.1
  26.8 4.3 %fusion = f32[64,1536]{1,0:T(8,128)S(1)} fusion(f32[8,1536]{1,0:T(8,128)S(1)} %fusion.93, f32[8,64,64]{2,1,0:T(8,128)} %constant.59.clone, f32[1536,64]{1,0:T(8,128)} %gather_fusion.1, pred[1536]{0:T(1024)(128)(4,1)S(1)} %compare_and_fusion, pred[1536]{0:T(1024)(128)(4,1)S(1)} %lt.28), kind=kOutput, calls=%fused_computation.15 | convolution fusion | flops 605650944 | bytes 969728 | tf_op jit(solution)/shard_map/vpq,qx->vpx/dot_general | solution.py:139
  31.1 1.4 fusion.54
  32.6 1.4 fusion.39
  35.9 1.8 fusion.6
  41.7 1.6 convolution_bitcast_fusion.15
  44.5 1.6 gather_fusion.2
  48.0 16.3 %collective-permute-start.4 = (f32[64,128]{0,1:T(8,128)}, f32[64,128]{0,1:T(8,128)}, u32[]{:S(2)}, u32[]{:S(2)}) collective-permute-start(f32[64,128]{0,1:T(8,128)} %get-tuple-element.35), channel_id=1, source_target_pairs={{0,1},{2,3},{4,5},{6,7},{8,9},{10,11},{12,13},{14,15},{16,17},{18,... | collective-permute-start | bytes 98312 | tf_op jit(solution)/shard_map/ppermute | solution.py:31
  65.6 1.9 convolution_bitcast_fusion.14
  68.0 5.2 %collective-permute-start.6 = (f32[64,128]{0,1:T(8,128)}, f32[64,128]{0,1:T(8,128)}, u32[]{:S(2)}, u32[]{:S(2)}) collective-permute-start(f32[64,128]{0,1:T(8,128)} %get-tuple-element.33), channel_id=1, source_target_pairs={{0,2},{2,4},{4,6},{6,8},{8,10},{10,12},{12,14},{14,16},{16,18},{18... | collective-permute-start | bytes 98312 | tf_op jit(solution)/shard_map/ppermute | solution.py:31
  73.2 5.2 %psum.56 = f32[8]{0:T(128)S(1)} all-reduce(f32[8]{0:T(128)S(1)} %convolution_bitcast_fusion.20), channel_id=1, replica_groups=mesh['region'=16,'sub'=2] {'sub'}, use_global_device_ids=true, to_apply=%region_2.5 | all-reduce | flops 8 | bytes 64 | tf_op jit(solution)/shard_map/psum | solution.py:147
  79.7 34.2 %psum.57 = f32[8]{0:T(128)S(1)} all-reduce(f32[8]{0:T(128)S(1)} %psum.56), channel_id=1, replica_groups=mesh['region'=16,'sub'=2] {'region'}, use_global_device_ids=true, to_apply=%region_3.6 | all-reduce | flops 8 | bytes 64 | tf_op jit(solution)/shard_map/psum | solution.py:147
  114.2 2.2 fusion.68
  119.1 3.7 gather_fusion.3
  122.8 4.3 %fusion.1 = f32[64,1536]{1,0:T(8,128)S(1)} fusion(f32[8,1536]{1,0:T(8,128)S(1)} %copy-done.38, f32[8,64,64]{2,1,0:T(8,128)} %constant.59.clone, f32[1536,64]{1,0:T(8,128)} %gather_fusion.3, pred[1536]{0:T(1024)(128)(4,1)S(1)} %copy-done.60, pred[1536]{0:T(1024)(128)(4,1)S(1)} %copy-done.65), kind=kOutput, calls=%fused_computation.16 | convolution fusion | flops 605650944 | bytes 969728 | tf_op jit(solution)/shard_map/vpq,qx->vpx/dot_general | solution.py:139
  127.1 1.4 fusion.51
  128.6 1.7 multiply_add_fusion.2
  132.2 1.8 fusion.8
  137.4 1.6 convolution_bitcast_fusion.13
  139.0 2.2 copy.118
  141.1 2.8 gather_fusion.4
  145.8 4.7 %collective-permute-start.8 = (f32[64,128]{0,1:T(8,128)}, f32[64,128]{0,1:T(8,128)}, u32[]{:S(2)}, u32[]{:S(2)}) collective-permute-start(f32[64,128]{0,1:T(8,128)} %get-tuple-element.31), channel_id=1, source_target_pairs={{0,1},{2,3},{4,5},{6,7},{8,9},{10,11},{12,13},{14,15},{16,17},{18,... | collective-permute-start | bytes 98312 | tf_op jit(solution)/shard_map/ppermute | solution.py:31
  150.5 1.7 collective-permute-start.9
  154.9 5.5 %psum.58 = f32[8]{0:T(128)S(1)} all-reduce(f32[8]{0:T(128)S(1)} %convolution_bitcast_fusion.19), channel_id=1, replica_groups=mesh['region'=16,'sub'=2] {'sub'}, use_global_device_ids=true, to_apply=%region_5.8 | all-reduce | flops 8 | bytes 64 | tf_op jit(solution)/shard_map/psum | solution.py:147
  161.7 30.6 %psum.59 = f32[8]{0:T(128)S(1)} all-reduce(f32[8]{0:T(128)S(1)} %psum.58), channel_id=1, replica_groups=mesh['region'=16,'sub'=2] {'region'}, use_global_device_ids=true, to_apply=%region_6.9 | all-reduce | flops 8 | bytes 64 | tf_op jit(solution)/shard_map/psum | solution.py:147
  193.2 3.0 fusion.66
  197.1 1.5 constant_dynamic-update-slice_fusion.13
  200.5 4.9 %gather_fusion.5 = f32[1536,64]{1,0:T(8,128)} fusion(f32[64,2048]{0,1:T(8,128)} %constant_dynamic-update-slice_fusion.10, s32[2048]{0:T(1024)S(1)} %pad_clamp_fusion), kind=kCustom, calls=%fused_computation.7.clone | custom fusion | bytes 792576 | tf_op jit(solution)/shard_map/jit(_take)/gather | solution.py:137
  205.4 4.3 %fusion.2 = f32[64,1536]{1,0:T(8,128)S(1)} fusion(f32[8,1536]{1,0:T(8,128)S(1)} %copy-done.38, f32[8,64,64]{2,1,0:T(8,128)} %constant.59.clone, f32[1536,64]{1,0:T(8,128)} %gather_fusion.5, pred[1536]{0:T(1024)(128)(4,1)S(1)} %copy-done.61, pred[1536]{0:T(1024)(128)(4,1)S(1)} %copy-done.66), kind=kOutput, calls=%fused_computation.17 | convolution fusion | flops 605650944 | bytes 969728 | tf_op jit(solution)/shard_map/vpq,qx->vpx/dot_general | solution.py:139
  209.8 1.4 fusion.48
  211.2 1.5 multiply_add_fusion.1
  214.6 1.8 fusion.10
  220.6 1.6 convolution_bitcast_fusion.11
  222.2 2.2 copy.120
  224.3 2.8 gather_fusion.6
  228.9 4.7 %collective-permute-start.12 = (f32[64,128]{0,1:T(8,128)}, f32[64,128]{0,1:T(8,128)}, u32[]{:S(2)}, u32[]{:S(2)}) collective-permute-start(f32[64,128]{0,1:T(8,128)} %get-tuple-element.27), channel_id=1, source_target_pairs={{0,1},{2,3},{4,5},{6,7},{8,9},{10,11},{12,13},{14,15},{16,17},{18,... | collective-permute-start | bytes 98312 | tf_op jit(solution)/shard_map/ppermute | solution.py:31
  233.6 1.5 collective-permute-start.13
  235.0 1.9 convolution_bitcast_fusion.10
  238.0 1.9 collective-permute-start.14
  239.9 5.6 %psum.60 = f32[8]{0:T(128)S(1)} all-reduce(f32[8]{0:T(128)} %convolution_bitcast_fusion.18), channel_id=1, replica_groups=mesh['region'=16,'sub'=2] {'sub'}, use_global_device_ids=true, to_apply=%region_8.11 | all-reduce | flops 8 | bytes 64 | tf_op jit(solution)/shard_map/psum | solution.py:147
  246.9 31.1 %psum.61 = f32[8]{0:T(128)} all-reduce(f32[8]{0:T(128)S(1)} %psum.60), channel_id=1, replica_groups=mesh['region'=16,'sub'=2] {'region'}, use_global_device_ids=true, to_apply=%region_9.12 | all-reduce | flops 8 | bytes 64 | tf_op jit(solution)/shard_map/psum | solution.py:147
  280.2 2.2 fusion.64
  283.3 1.5 constant_dynamic-update-slice_fusion.18
  285.4 1.5 constant_dynamic-update-slice_fusion.16
  286.9 1.5 constant_dynamic-update-slice_fusion.15
  288.4 4.9 %gather_fusion.7 = f32[1536,64]{1,0:T(8,128)} fusion(f32[64,2048]{0,1:T(8,128)} %constant_dynamic-update-slice_fusion.15, s32[2048]{0:T(1024)S(1)} %pad_clamp_fusion), kind=kCustom, calls=%fused_computation.8.clone | custom fusion | bytes 792576 | tf_op jit(solution)/shard_map/jit(_take)/gather | solution.py:137
  293.3 4.3 %fusion.3 = f32[64,1536]{1,0:T(8,128)S(1)} fusion(f32[8,1536]{1,0:T(8,128)S(1)} %copy-done.38, f32[8,64,64]{2,1,0:T(8,128)} %constant.59.clone, f32[1536,64]{1,0:T(8,128)} %gather_fusion.7, pred[1536]{0:T(1024)(128)(4,1)S(1)} %copy-done.62, pred[1536]{0:T(1024)(128)(4,1)S(1)} %copy-done.67), kind=kOutput, calls=%fused_computation.18 | convolution fusion | flops 605650944 | bytes 969728 | tf_op jit(solution)/shard_map/vpq,qx->vpx/dot_general | solution.py:139
  297.6 1.4 fusion.45
  299.1 1.5 multiply_add_fusion
  302.5 1.8 fusion.12
  312.1 4.1 %collective-permute-start.16 = (f32[64,128]{0,1:T(8,128)}, f32[64,128]{0,1:T(8,128)S(1)}, u32[]{:S(2)}, u32[]{:S(2)}) collective-permute-start(f32[64,128]{0,1:T(8,128)} %get-tuple-element.23), channel_id=1, source_target_pairs={{0,1},{2,3},{4,5},{6,7},{8,9},{10,11},{12,13},{14,15},{16,17},{18,... | collective-permute-start | bytes 98312 | tf_op jit(solution)/shard_map/ppermute | solution.py:31
  316.2 1.5 collective-permute-start.17
  317.7 1.9 convolution_bitcast_fusion.8
  320.2 1.9 collective-permute-start.18
  322.1 5.5 %psum.62 = f32[8]{0:T(128)S(1)} all-reduce(f32[8]{0:T(128)S(1)} %convolution_bitcast_fusion.17), channel_id=1, replica_groups=mesh['region'=16,'sub'=2] {'sub'}, use_global_device_ids=true, to_apply=%region_11.14 | all-reduce | flops 8 | bytes 64 | tf_op jit(solution)/shard_map/psum | solution.py:147
  328.9 30.6 %psum.63 = f32[8]{0:T(128)S(1)} all-reduce(f32[8]{0:T(128)S(1)} %psum.62), channel_id=1, replica_groups=mesh['region'=16,'sub'=2] {'region'}, use_global_device_ids=true, to_apply=%region_12.15 | all-reduce | flops 8 | bytes 64 | tf_op jit(solution)/shard_map/psum | solution.py:147
  359.7 2.2 fusion.62
  363.8 3.7 gather_fusion.9
  367.5 4.3 %fusion.4 = f32[64,1536]{1,0:T(8,128)S(1)} fusion(f32[8,1536]{1,0:T(8,128)S(1)} %copy-done.39, f32[8,64,64]{2,1,0:T(8,128)} %constant.59.clone, f32[1536,64]{1,0:T(8,128)} %gather_fusion.9, pred[1536]{0:T(1024)(128)(4,1)S(1)} %copy-done.63, pred[1536]{0:T(1024)(128)(4,1)S(1)} %copy-done.68), kind=kOutput, calls=%fused_computation.19 | convolution fusion | flops 605650944 | bytes 969728 | tf_op jit(solution)/shard_map/vpq,qx->vpx/dot_general | solution.py:139
  371.9 1.4 fusion.42
  (289 shorter events, 72.1 us)
Async XLA Ops:
  2.0 8.5 %copy-start.42 = (pred[512]{0:T(512)(128)(4,1)}, pred[512]{0:T(512)(128)(4,1)S(1)}, u32[]{:S(2)}) copy-start(pred[512]{0:T(512)(128)(4,1)S(1)} %compare_and_fusion.1) | copy-start | bytes 1540
  8.8 9.6 %copy-start.13 = (f32[64,6,256]{0,2,1:T(8,128)}, f32[64,6,256]{0,2,1:T(8,128)S(1)}, u32[]{:S(2)}) copy-start(f32[64,6,256]{0,2,1:T(8,128)S(1)} %copy.114) | copy-start | bytes 1179652
  10.5 10.8 %copy-start.41 = (s32[6,256]{1,0:T(8,128)S(1)}, s32[6,256]{1,0:T(8,128)}, u32[]{:S(2)}) copy-start(s32[6,256]{1,0:T(8,128)} %param.20) | copy-start | bytes 18436
  10.5 10.8 %copy-start.52 = (s32[6,256]{1,0:T(8,128)S(1)}, s32[6,256]{1,0:T(8,128)}, u32[]{:S(2)}) copy-start(s32[6,256]{1,0:T(8,128)} %param.21) | copy-start | bytes 18436
  10.5 10.9 %copy-start.53 = (f32[6,256]{1,0:T(8,128)S(1)}, f32[6,256]{1,0:T(8,128)}, u32[]{:S(2)}) copy-start(f32[6,256]{1,0:T(8,128)} %param.18) | copy-start | bytes 18436
  10.5 10.9 %copy-start.54 = (s32[6,256]{1,0:T(8,128)S(1)}, s32[6,256]{1,0:T(8,128)}, u32[]{:S(2)}) copy-start(s32[6,256]{1,0:T(8,128)} %param.22) | copy-start | bytes 18436
  10.7 11.4 %collective-permute-start = (f32[64,128]{0,1:T(8,128)S(1)}, f32[64,128]{0,1:T(8,128)S(1)}, u32[]{:S(2)}, u32[]{:S(2)}) collective-permute-start(f32[64,128]{0,1:T(8,128)S(1)} %get-tuple-element.39), channel_id=1, source_target_pairs={{0,1},{2,3},{4,5},{6,7},{8,9},{10,11},{12,13},{14,15},{16,17},{18,... | collective-permute-start | bytes 98312 | tf_op jit(solution)/shard_map/ppermute | solution.py:31
  15.6 6.5 %collective-permute-start.1 = (f32[64,128]{0,1:T(8,128)S(1)}, f32[64,128]{0,1:T(8,128)S(1)}, u32[]{:S(2)}, u32[]{:S(2)}) collective-permute-start(f32[64,128]{0,1:T(8,128)S(1)} %get-tuple-element.38), channel_id=1, source_target_pairs={{1,0},{3,2},{5,4},{7,6},{9,8},{11,10},{13,12},{15,14},{17,16},{19,... | collective-permute-start | bytes 98312 | tf_op jit(solution)/shard_map/ppermute | solution.py:32
  16.9 5.2 %collective-permute-start.2 = (f32[64,128]{0,1:T(8,128)S(1)}, f32[64,128]{0,1:T(8,128)S(1)}, u32[]{:S(2)}, u32[]{:S(2)}) collective-permute-start(f32[64,128]{0,1:T(8,128)S(1)} %get-tuple-element.37), channel_id=1, source_target_pairs={{0,2},{2,4},{4,6},{6,8},{8,10},{10,12},{12,14},{14,16},{16,18},{18... | collective-permute-start | bytes 98312 | tf_op jit(solution)/shard_map/ppermute | solution.py:31
  18.4 4.7 %collective-permute-start.3 = (f32[64,128]{0,1:T(8,128)S(1)}, f32[64,128]{0,1:T(8,128)S(1)}, u32[]{:S(2)}, u32[]{:S(2)}) collective-permute-start(f32[64,128]{0,1:T(8,128)S(1)} %get-tuple-element.36), channel_id=1, source_target_pairs={{2,0},{4,2},{6,4},{8,6},{10,8},{12,10},{14,12},{16,14},{18,16},{20... | collective-permute-start | bytes 98312 | tf_op jit(solution)/shard_map/ppermute | solution.py:32
  21.3 5.5 %copy-start.59 = (pred[1536]{0:T(1024)(128)(4,1)}, pred[1536]{0:T(1024)(128)(4,1)S(1)}, u32[]{:S(2)}) copy-start(pred[1536]{0:T(1024)(128)(4,1)S(1)} %compare_and_fusion) | copy-start | bytes 4612
  21.4 5.4 %copy-start.37 = (f32[8,1536]{1,0:T(8,128)}, f32[8,1536]{1,0:T(8,128)S(1)}, u32[]{:S(2)}) copy-start(f32[8,1536]{1,0:T(8,128)S(1)} %fusion.93) | copy-start | bytes 147460
  21.4 5.4 %copy-start.64 = (pred[1536]{0:T(1024)(128)(4,1)}, pred[1536]{0:T(1024)(128)(4,1)S(1)}, u32[]{:S(2)}) copy-start(pred[1536]{0:T(1024)(128)(4,1)S(1)} %lt.28) | copy-start | bytes 4612
  26.8 5.7 %copy-start.17 = (f32[8,8,8,256]{3,0,2,1:T(8,128)S(1)}, f32[8,8,8,256]{3,0,2,1:T(8,128)}, u32[]{:S(2)}) copy-start(f32[8,8,8,256]{3,0,2,1:T(8,128)} %copy-done.16) | copy-start | bytes 1572868
  26.8 5.7 %copy-start.25 = (f32[8,8,8,256]{3,2,1,0:T(8,128)S(1)}, f32[8,8,8,256]{3,2,1,0:T(8,128)}, u32[]{:S(2)}) copy-start(f32[8,8,8,256]{3,2,1,0:T(8,128)} %param.16) | copy-start | bytes 1572868
  44.5 22.9 %copy-start.9 = (f32[64,6,256]{0,2,1:T(8,128)}, f32[64,6,256]{0,2,1:T(8,128)S(1)}, u32[]{:S(2)}) copy-start(f32[64,6,256]{0,2,1:T(8,128)S(1)} %copy.116) | copy-start | bytes 1179652
  47.3 20.2 %copy-start.48 = (f32[64,1]{0,1:T(1,128)S(1)}, f32[64,1]{0,1:T(1,128)}, u32[]{:S(2)}) copy-start(f32[64,1]{0,1:T(1,128)} %constant.64) | copy-start | bytes 772
  48.0 19.9 %copy-start.55 = (s32[1536]{0:T(1024)S(1)}, s32[1536]{0:T(1024)}, u32[]{:S(2)}) copy-start(s32[1536]{0:T(1024)} %eq.38) | copy-start | bytes 18436
  48.0 66.0 %copy-start.69 = (f32[8]{0:T(128)S(1)}, f32[8]{0:T(128)}, u32[]{:S(2)}) copy-start(f32[8]{0:T(128)} %param.19) | copy-start | bytes 100
  48.0 66.2 %copy-start.45 = (f32[64]{0:T(128)S(1)}, f32[64]{0:T(128)}, u32[]{:S(2)}) copy-start(f32[64]{0:T(128)} %constant.32.clone) | copy-start | bytes 772
  48.0 68.5 %collective-permute-start.4 = (f32[64,128]{0,1:T(8,128)}, f32[64,128]{0,1:T(8,128)}, u32[]{:S(2)}, u32[]{:S(2)}) collective-permute-start(f32[64,128]{0,1:T(8,128)} %get-tuple-element.35), channel_id=1, source_target_pairs={{0,1},{2,3},{4,5},{6,7},{8,9},{10,11},{12,13},{14,15},{16,17},{18,... | collective-permute-start | bytes 98312 | tf_op jit(solution)/shard_map/ppermute | solution.py:31
  64.3 53.1 %collective-permute-start.5 = (f32[64,128]{0,1:T(8,128)}, f32[64,128]{0,1:T(8,128)S(1)}, u32[]{:S(2)}, u32[]{:S(2)}) collective-permute-start(f32[64,128]{0,1:T(8,128)} %get-tuple-element.34), channel_id=1, source_target_pairs={{1,0},{3,2},{5,4},{7,6},{9,8},{11,10},{13,12},{15,14},{17,16},{19,... | collective-permute-start | bytes 98312 | tf_op jit(solution)/shard_map/ppermute | solution.py:32
  68.0 49.4 %collective-permute-start.6 = (f32[64,128]{0,1:T(8,128)}, f32[64,128]{0,1:T(8,128)}, u32[]{:S(2)}, u32[]{:S(2)}) collective-permute-start(f32[64,128]{0,1:T(8,128)} %get-tuple-element.33), channel_id=1, source_target_pairs={{0,2},{2,4},{4,6},{6,8},{8,10},{10,12},{12,14},{14,16},{16,18},{18... | collective-permute-start | bytes 98312 | tf_op jit(solution)/shard_map/ppermute | solution.py:31
  78.4 39.8 %collective-permute-start.7 = (f32[64,128]{0,1:T(8,128)}, f32[64,128]{0,1:T(8,128)}, u32[]{:S(2)}, u32[]{:S(2)}) collective-permute-start(f32[64,128]{0,1:T(8,128)} %get-tuple-element.32), channel_id=1, source_target_pairs={{2,0},{4,2},{6,4},{8,6},{10,8},{12,10},{14,12},{16,14},{18,16},{20... | collective-permute-start | bytes 98312 | tf_op jit(solution)/shard_map/ppermute | solution.py:32
  122.7 5.8 %copy-start.3 = (f32[8,8,8,256]{3,0,2,1:T(8,128)S(1)}, f32[8,8,8,256]{3,0,2,1:T(8,128)}, u32[]{:S(2)}) copy-start(f32[8,8,8,256]{3,0,2,1:T(8,128)} %get-tuple-element.17) | copy-start | bytes 1572868
  122.8 5.8 %copy-start.15 = (f32[8,8,8,256]{3,0,2,1:T(8,128)S(1)}, f32[8,8,8,256]{3,0,2,1:T(8,128)}, u32[]{:S(2)}) copy-start(f32[8,8,8,256]{3,0,2,1:T(8,128)} %copy-done.14) | copy-start | bytes 1572868
  122.8 5.8 %copy-start.26 = (f32[8,8,8,256]{3,2,1,0:T(8,128)S(1)}, f32[8,8,8,256]{3,2,1,0:T(8,128)}, u32[]{:S(2)}) copy-start(f32[8,8,8,256]{3,2,1,0:T(8,128)} %param.16) | copy-start | bytes 1572868
  122.8 5.8 %copy-start.27 = (f32[512,256,1]{1,0,2:T(8,128)S(1)}, f32[512,256,1]{1,0,2:T(8,128)}, u32[]{:S(2)}) copy-start(f32[512,256,1]{1,0,2:T(8,128)} %fusion.68) | copy-start | bytes 1572868
  141.1 11.0 %copy-start.28 = (f32[8,8,8,256]{3,2,1,0:T(8,128)S(1)}, f32[8,8,8,256]{3,2,1,0:T(8,128)}, u32[]{:S(2)}) copy-start(f32[8,8,8,256]{3,2,1,0:T(8,128)} %copy.69) | copy-start | bytes 1572868
  145.1 8.0 %copy-start.49 = (f32[64,1]{0,1:T(1,128)S(1)}, f32[64,1]{0,1:T(1,128)}, u32[]{:S(2)}) copy-start(f32[64,1]{0,1:T(1,128)} %constant.64) | copy-start | bytes 772
  145.8 7.6 %copy-start.56 = (s32[1536]{0:T(1024)S(1)}, s32[1536]{0:T(1024)}, u32[]{:S(2)}) copy-start(s32[1536]{0:T(1024)} %eq.38) | copy-start | bytes 18436
  145.8 51.4 %collective-permute-start.8 = (f32[64,128]{0,1:T(8,128)}, f32[64,128]{0,1:T(8,128)}, u32[]{:S(2)}, u32[]{:S(2)}) collective-permute-start(f32[64,128]{0,1:T(8,128)} %get-tuple-element.31), channel_id=1, source_target_pairs={{0,1},{2,3},{4,5},{6,7},{8,9},{10,11},{12,13},{14,15},{16,17},{18,... | collective-permute-start | bytes 98312 | tf_op jit(solution)/shard_map/ppermute | solution.py:31
  150.5 48.1 %collective-permute-start.9 = (f32[64,128]{0,1:T(8,128)}, f32[64,128]{0,1:T(8,128)S(1)}, u32[]{:S(2)}, u32[]{:S(2)}) collective-permute-start(f32[64,128]{0,1:T(8,128)} %get-tuple-element.30), channel_id=1, source_target_pairs={{1,0},{3,2},{5,4},{7,6},{9,8},{11,10},{13,12},{15,14},{17,16},{19,... | collective-permute-start | bytes 98312 | tf_op jit(solution)/shard_map/ppermute | solution.py:32
  153.5 45.7 %collective-permute-start.10 = (f32[64,128]{0,1:T(8,128)}, f32[64,128]{0,1:T(8,128)S(1)}, u32[]{:S(2)}, u32[]{:S(2)}) collective-permute-start(f32[64,128]{0,1:T(8,128)} %get-tuple-element.29), channel_id=1, source_target_pairs={{0,2},{2,4},{4,6},{6,8},{8,10},{10,12},{12,14},{14,16},{16,18},{18... | collective-permute-start | bytes 98312 | tf_op jit(solution)/shard_map/ppermute | solution.py:31
  160.4 39.4 %collective-permute-start.11 = (f32[64,128]{0,1:T(8,128)}, f32[64,128]{0,1:T(8,128)S(1)}, u32[]{:S(2)}, u32[]{:S(2)}) collective-permute-start(f32[64,128]{0,1:T(8,128)} %get-tuple-element.28), channel_id=1, source_target_pairs={{2,0},{4,2},{6,4},{8,6},{10,8},{12,10},{14,12},{16,14},{18,16},{20... | collective-permute-start | bytes 98312 | tf_op jit(solution)/shard_map/ppermute | solution.py:32
  205.4 5.8 %copy-start.4 = (f32[8,8,8,256]{3,0,2,1:T(8,128)S(1)}, f32[8,8,8,256]{3,0,2,1:T(8,128)}, u32[]{:S(2)}) copy-start(f32[8,8,8,256]{3,0,2,1:T(8,128)} %get-tuple-element.17) | copy-start | bytes 1572868
  205.4 5.8 %copy-start.21 = (f32[8,8,8,256]{3,0,2,1:T(8,128)S(1)}, f32[8,8,8,256]{3,0,2,1:T(8,128)}, u32[]{:S(2)}) copy-start(f32[8,8,8,256]{3,0,2,1:T(8,128)} %copy-done.20) | copy-start | bytes 1572868
  205.4 5.8 %copy-start.29 = (f32[8,8,8,256]{3,0,2,1:T(8,128)S(1)}, f32[8,8,8,256]{3,0,2,1:T(8,128)}, u32[]{:S(2)}) copy-start(f32[8,8,8,256]{3,0,2,1:T(8,128)} %get-tuple-element.15) | copy-start | bytes 1572868
  205.4 5.8 %copy-start.31 = (f32[512,256,1]{1,0,2:T(8,128)S(1)}, f32[512,256,1]{1,0,2:T(8,128)}, u32[]{:S(2)}) copy-start(f32[512,256,1]{1,0,2:T(8,128)} %fusion.66) | copy-start | bytes 1572868
  228.2 8.8 %copy-start.50 = (f32[64,1]{0,1:T(1,128)S(1)}, f32[64,1]{0,1:T(1,128)}, u32[]{:S(2)}) copy-start(f32[64,1]{0,1:T(1,128)} %constant.64) | copy-start | bytes 772
  228.9 8.4 %copy-start.57 = (s32[1536]{0:T(1024)S(1)}, s32[1536]{0:T(1024)}, u32[]{:S(2)}) copy-start(s32[1536]{0:T(1024)} %eq.38) | copy-start | bytes 18436
  228.9 51.3 %copy-start.46 = (f32[64]{0:T(128)S(1)}, f32[64]{0:T(128)}, u32[]{:S(2)}) copy-start(f32[64]{0:T(128)} %constant.32.clone) | copy-start | bytes 772
  228.9 54.4 %collective-permute-start.12 = (f32[64,128]{0,1:T(8,128)}, f32[64,128]{0,1:T(8,128)}, u32[]{:S(2)}, u32[]{:S(2)}) collective-permute-start(f32[64,128]{0,1:T(8,128)} %get-tuple-element.27), channel_id=1, source_target_pairs={{0,1},{2,3},{4,5},{6,7},{8,9},{10,11},{12,13},{14,15},{16,17},{18,... | collective-permute-start | bytes 98312 | tf_op jit(solution)/shard_map/ppermute | solution.py:31
  233.6 51.2 %collective-permute-start.13 = (f32[64,128]{0,1:T(8,128)}, f32[64,128]{0,1:T(8,128)S(1)}, u32[]{:S(2)}, u32[]{:S(2)}) collective-permute-start(f32[64,128]{0,1:T(8,128)} %get-tuple-element.26), channel_id=1, source_target_pairs={{1,0},{3,2},{5,4},{7,6},{9,8},{11,10},{13,12},{15,14},{17,16},{19,... | collective-permute-start | bytes 98312 | tf_op jit(solution)/shard_map/ppermute | solution.py:32
  238.0 47.4 %collective-permute-start.14 = (f32[64,128]{0,1:T(8,128)}, f32[64,128]{0,1:T(8,128)}, u32[]{:S(2)}, u32[]{:S(2)}) collective-permute-start(f32[64,128]{0,1:T(8,128)} %get-tuple-element.25), channel_id=1, source_target_pairs={{0,2},{2,4},{4,6},{6,8},{8,10},{10,12},{12,14},{14,16},{16,18},{18... | collective-permute-start | bytes 98312 | tf_op jit(solution)/shard_map/ppermute | solution.py:31
  245.6 41.3 %collective-permute-start.15 = (f32[64,128]{0,1:T(8,128)}, f32[64,128]{0,1:T(8,128)}, u32[]{:S(2)}, u32[]{:S(2)}) collective-permute-start(f32[64,128]{0,1:T(8,128)} %get-tuple-element.24), channel_id=1, source_target_pairs={{2,0},{4,2},{6,4},{8,6},{10,8},{12,10},{14,12},{16,14},{18,16},{20... | collective-permute-start | bytes 98312 | tf_op jit(solution)/shard_map/ppermute | solution.py:32
  293.3 5.8 %copy-start.5 = (f32[8,8,8,256]{3,0,2,1:T(8,128)S(1)}, f32[8,8,8,256]{3,0,2,1:T(8,128)}, u32[]{:S(2)}) copy-start(f32[8,8,8,256]{3,0,2,1:T(8,128)} %get-tuple-element.17) | copy-start | bytes 1572868
  293.3 5.8 %copy-start.23 = (f32[8,8,8,256]{3,0,2,1:T(8,128)S(1)}, f32[8,8,8,256]{3,0,2,1:T(8,128)}, u32[]{:S(2)}) copy-start(f32[8,8,8,256]{3,0,2,1:T(8,128)} %copy-done.22) | copy-start | bytes 1572868
  293.3 5.8 %copy-start.32 = (f32[512,256,1]{1,0,2:T(8,128)S(1)}, f32[512,256,1]{1,0,2:T(8,128)}, u32[]{:S(2)}) copy-start(f32[512,256,1]{1,0,2:T(8,128)} %fusion.64) | copy-start | bytes 1572868
  293.3 5.8 %copy-start.34 = (f32[8,8,8,256]{3,0,2,1:T(8,128)S(1)}, f32[8,8,8,256]{3,0,2,1:T(8,128)}, u32[]{:S(2)}) copy-start(f32[8,8,8,256]{3,0,2,1:T(8,128)} %get-tuple-element.13) | copy-start | bytes 1572868
  309.4 10.2 %copy-start.7 = (f32[64,6,256]{0,2,1:T(8,128)}, f32[64,6,256]{0,2,1:T(8,128)S(1)}, u32[]{:S(2)}) copy-start(f32[64,6,256]{0,2,1:T(8,128)S(1)} %copy.122) | copy-start | bytes 1179652
  311.4 8.3 %copy-start.51 = (f32[64,1]{0,1:T(1,128)S(1)}, f32[64,1]{0,1:T(1,128)}, u32[]{:S(2)}) copy-start(f32[64,1]{0,1:T(1,128)} %constant.64) | copy-start | bytes 772
  312.1 7.9 %copy-start.58 = (s32[1536]{0:T(1024)S(1)}, s32[1536]{0:T(1024)}, u32[]{:S(2)}) copy-start(s32[1536]{0:T(1024)} %eq.38) | copy-start | bytes 18436
  312.1 47.4 %copy-start.70 = (f32[8]{0:T(128)S(1)}, f32[8]{0:T(128)}, u32[]{:S(2)}) copy-start(f32[8]{0:T(128)} %param.19) | copy-start | bytes 100
  312.1 47.6 %copy-start.47 = (f32[64]{0:T(128)S(1)}, f32[64]{0:T(128)}, u32[]{:S(2)}) copy-start(f32[64]{0:T(128)} %constant.32.clone) | copy-start | bytes 772
  312.1 49.9 %collective-permute-start.16 = (f32[64,128]{0,1:T(8,128)}, f32[64,128]{0,1:T(8,128)S(1)}, u32[]{:S(2)}, u32[]{:S(2)}) collective-permute-start(f32[64,128]{0,1:T(8,128)} %get-tuple-element.23), channel_id=1, source_target_pairs={{0,1},{2,3},{4,5},{6,7},{8,9},{10,11},{12,13},{14,15},{16,17},{18,... | collective-permute-start | bytes 98312 | tf_op jit(solution)/shard_map/ppermute | solution.py:31
  316.2 45.8 %collective-permute-start.17 = (f32[64,128]{0,1:T(8,128)}, f32[64,128]{0,1:T(8,128)S(1)}, u32[]{:S(2)}, u32[]{:S(2)}) collective-permute-start(f32[64,128]{0,1:T(8,128)} %get-tuple-element.22), channel_id=1, source_target_pairs={{1,0},{3,2},{5,4},{7,6},{9,8},{11,10},{13,12},{15,14},{17,16},{19,... | collective-permute-start | bytes 98312 | tf_op jit(solution)/shard_map/ppermute | solution.py:32
  320.2 41.9 %collective-permute-start.18 = (f32[64,128]{0,1:T(8,128)}, f32[64,128]{0,1:T(8,128)}, u32[]{:S(2)}, u32[]{:S(2)}) collective-permute-start(f32[64,128]{0,1:T(8,128)} %get-tuple-element.21), channel_id=1, source_target_pairs={{0,2},{2,4},{4,6},{6,8},{8,10},{10,12},{12,14},{14,16},{16,18},{18... | collective-permute-start | bytes 98312 | tf_op jit(solution)/shard_map/ppermute | solution.py:31
  327.6 35.3 %collective-permute-start.19 = (f32[64,128]{0,1:T(8,128)}, f32[64,128]{0,1:T(8,128)}, u32[]{:S(2)}, u32[]{:S(2)}) collective-permute-start(f32[64,128]{0,1:T(8,128)} %get-tuple-element.20), channel_id=1, source_target_pairs={{2,0},{4,2},{6,4},{8,6},{10,8},{12,10},{14,12},{16,14},{18,16},{20... | collective-permute-start | bytes 98312 | tf_op jit(solution)/shard_map/ppermute | solution.py:32
  367.5 5.8 %copy-start.2 = (f32[8,8,8,256]{3,0,2,1:T(8,128)S(1)}, f32[8,8,8,256]{3,0,2,1:T(8,128)}, u32[]{:S(2)}) copy-start(f32[8,8,8,256]{3,0,2,1:T(8,128)} %copy-done.1) | copy-start | bytes 1572868
  367.5 5.8 %copy-start.6 = (f32[8,8,8,256]{3,0,2,1:T(8,128)S(1)}, f32[8,8,8,256]{3,0,2,1:T(8,128)}, u32[]{:S(2)}) copy-start(f32[8,8,8,256]{3,0,2,1:T(8,128)} %get-tuple-element.17) | copy-start | bytes 1572868
  367.5 5.8 %copy-start.19 = (f32[8,8,8,256]{3,0,2,1:T(8,128)S(1)}, f32[8,8,8,256]{3,0,2,1:T(8,128)}, u32[]{:S(2)}) copy-start(f32[8,8,8,256]{3,0,2,1:T(8,128)} %copy-done.18) | copy-start | bytes 1572868
  367.5 5.8 %copy-start.30 = (f32[512,256,1]{1,0,2:T(8,128)S(1)}, f32[512,256,1]{1,0,2:T(8,128)}, u32[]{:S(2)}) copy-start(f32[512,256,1]{1,0,2:T(8,128)} %fusion.62) | copy-start | bytes 1572868
  367.5 5.8 %copy-start.33 = (f32[8,8,8,256]{3,0,2,1:T(8,128)S(1)}, f32[8,8,8,256]{3,0,2,1:T(8,128)}, u32[]{:S(2)}) copy-start(f32[8,8,8,256]{3,0,2,1:T(8,128)} %get-tuple-element.11) | copy-start | bytes 1572868
  (27 other events, 80.5 us)
